TPU v7x, 128 devices: a whole 4x4x4 slice. The times are simulated.
128 devices in a mesh: dp: 8 (over x, y_lo), expert: 16 (over z, y_hi, core).
Axes of the slice: x: 4, y: 4 (y_hi: 2, y_lo: 2; y = y_hi * 2 + y_lo), z: 4, core: 2. Of those that a mesh axis runs over, the one named last changes fastest.
Arguments:
- tokens: bfloat16 [32768, 1536], P(('dp', 'expert')), may hold values from -24 to 24
- cotangent: bfloat16 [32768, 1536], P(('dp', 'expert')), may hold values from -0.59765625 to 0.59765625
- chosen: int32 [512, 16, 8], P(('dp', 'expert')), may hold values from 0 to 63, as said below
- w_router: bfloat16 [1536, 16], replicated, may hold values from -0.15625 to 0.15625
- w_gate: bfloat16 [16, 1536, 1024], P('expert', 'dp'), may hold values from -0.15625 to 0.15625
- w_up: bfloat16 [16, 1536, 1024], P('expert', 'dp'), may hold values from -0.15625 to 0.15625
- w_down: bfloat16 [16, 1024, 1536], P('expert', 'dp'), may hold values from -0.1875 to 0.1875
Outputs:
- mixed: bfloat16 [32768, 1536], P(('dp', 'expert'))
- grad_tokens: bfloat16 [32768, 1536], P(('dp', 'expert'))
- grad_gate: float32 [16, 1536, 1024], P('expert', 'dp')
- grad_up: float32 [16, 1536, 1024], P('expert', 'dp')
- down_weight_gradient: float32 [16, 1024, 1536], P('expert', 'dp')
- grad_router: float32 [1536, 16], replicated
Inputs may be any that keep to these rules, and one draw needn't show every extreme that they name: `chosen`: for each aligned block of 64 token rows and each expert, 8 different row numbers within the block; so every device has exactly 32 slots for each expert.
All inputs are finite; a program needn't handle non-finite values.
Results may differ from a plain program's by a relative error of at most 0.017.
Values may be sent and summed in bfloat16 or wider, within the bound.
A program may use at most 128 MiB of HBM per device.

v0:
```python
import jax
import jax.numpy as jnp
from jax import lax
from jax.sharding import PartitionSpec as P


def to_blocks(slot_array, num_blocks, pick_count):
    expert_count = slot_array.shape[0]
    trailing = slot_array.shape[2:]
    grouped = slot_array.reshape((expert_count, num_blocks, pick_count) + trailing)
    axis_order = (1, 0, 2) + tuple(range(3, 3 + len(trailing)))
    return jnp.transpose(grouped, axis_order).reshape(
        (num_blocks, expert_count * pick_count) + trailing
    )


def weight_grads(expert_rows, hidden, expert_cot, d_pre_gate, d_pre_up):
    hidden_activations = hidden.shape[2]
    both_grads = jnp.concatenate([d_pre_gate, d_pre_up], axis=2)
    columns = expert_rows
    in_share = lax.psum_scatter(
        jnp.einsum("erc,erk->cek", columns, both_grads, preferred_element_type=jnp.float32).astype(
            jnp.bfloat16
        ),
        "dp",
        scatter_dimension=0,
        tiled=True,
    ).astype(jnp.float32)
    grad_gate = jnp.transpose(in_share[:, :, :hidden_activations], (1, 0, 2))
    grad_up = jnp.transpose(in_share[:, :, hidden_activations:], (1, 0, 2))
    columns = hidden
    out_share = lax.psum_scatter(
        jnp.einsum("erc,erd->ced", columns, expert_cot, preferred_element_type=jnp.float32).astype(
            jnp.bfloat16
        ),
        "dp",
        scatter_dimension=0,
        tiled=True,
    ).astype(jnp.float32)
    down_weight_gradient = jnp.transpose(out_share, (1, 0, 2))
    return (grad_gate, grad_up, down_weight_gradient)


def body(tokens, cotangent, chosen, w_router, w_gate, w_up, w_down):
    tok_rows, model_width = tokens.shape
    num_blocks, expert_count, pick_count = chosen.shape
    block_rows = tok_rows // num_blocks
    slot_count = num_blocks * pick_count
    logits = jnp.dot(tokens, w_router, preferred_element_type=jnp.float32)
    gate_values = jax.nn.sigmoid(logits)
    offsets = (jnp.arange(num_blocks, dtype=jnp.int32) * block_rows)[:, None, None]
    slot_rows = jnp.transpose(chosen + offsets, (1, 0, 2)).reshape(expert_count, slot_count)
    picked = tokens[slot_rows]
    slot_gate_values = jnp.take_along_axis(gate_values.T, slot_rows, axis=1)
    cot_rows = cotangent[slot_rows]
    scaled_cot = (slot_gate_values[:, :, None] * cot_rows.astype(jnp.float32)).astype(jnp.bfloat16)
    full_gate, full_up, full_down = (
        lax.all_gather(w_gate, "dp", axis=1, tiled=True),
        lax.all_gather(w_up, "dp", axis=1, tiled=True),
        lax.all_gather(w_down, "dp", axis=1, tiled=True),
    )
    expert_rows = lax.all_to_all(picked, "expert", split_axis=0, concat_axis=1, tiled=True)
    pre_gate = jnp.einsum(
        "erd,edh->erh", expert_rows, full_gate, preferred_element_type=jnp.float32
    )
    pre_up = jnp.einsum("erd,edh->erh", expert_rows, full_up, preferred_element_type=jnp.float32)
    silu_gate = jax.nn.silu(pre_gate)
    hidden = (silu_gate * pre_up).astype(jnp.bfloat16)
    expert_out = jnp.einsum(
        "erh,ehd->erd", hidden, full_down, preferred_element_type=jnp.float32
    ).astype(jnp.bfloat16)
    returned = lax.all_to_all(expert_out, "expert", split_axis=1, concat_axis=0, tiled=True)
    expert_cot = lax.all_to_all(scaled_cot, "expert", split_axis=0, concat_axis=1, tiled=True)
    back_gate, back_up, back_down = (full_gate, full_up, full_down)
    d_hidden = jnp.einsum("erd,ehd->erh", expert_cot, back_down, preferred_element_type=jnp.float32)
    gate_sigmoid = jax.nn.sigmoid(pre_gate)
    d_pre_gate = (
        d_hidden * pre_up * gate_sigmoid * (1.0 + pre_gate * (1.0 - gate_sigmoid))
    ).astype(jnp.bfloat16)
    d_pre_up = (d_hidden * silu_gate).astype(jnp.bfloat16)
    d_rows = (
        jnp.einsum("erh,edh->erd", d_pre_gate, back_gate, preferred_element_type=jnp.float32)
        + jnp.einsum("erh,edh->erd", d_pre_up, back_up, preferred_element_type=jnp.float32)
    ).astype(jnp.bfloat16)
    row_grads = lax.all_to_all(d_rows, "expert", split_axis=1, concat_axis=0, tiled=True)
    position_hits = chosen[:, :, :, None] == jnp.arange(block_rows, dtype=jnp.int32)
    indicator_matrix = position_hits.reshape(num_blocks, expert_count * pick_count, block_rows)
    gate_weighted_rows = to_blocks(slot_gate_values, num_blocks, pick_count)[
        :, :, None
    ] * to_blocks(returned, num_blocks, pick_count).astype(jnp.float32)
    mixed = (
        jnp.einsum(
            "wze,wzi->wei",
            indicator_matrix.astype(jnp.float32),
            gate_weighted_rows,
            precision=lax.Precision.HIGHEST,
        )
        .reshape(tok_rows, model_width)
        .astype(jnp.bfloat16)
    )
    slot_dots = jnp.sum(cot_rows.astype(jnp.float32) * returned.astype(jnp.float32), axis=2)
    dgate = jnp.einsum(
        "bept,ebp->bte",
        position_hits.astype(jnp.float32),
        slot_dots.reshape(expert_count, num_blocks, pick_count),
        precision=lax.Precision.HIGHEST,
    ).reshape(tok_rows, expert_count)
    d_logit = (dgate * gate_values * (1.0 - gate_values)).astype(jnp.bfloat16)
    gathered_grads = jnp.einsum(
        "wze,wzi->wei",
        indicator_matrix.astype(jnp.bfloat16),
        to_blocks(row_grads, num_blocks, pick_count),
        preferred_element_type=jnp.float32,
    ).reshape(tok_rows, model_width)
    grad_tokens = (
        gathered_grads + jnp.dot(d_logit, w_router.T, preferred_element_type=jnp.float32)
    ).astype(jnp.bfloat16)
    grad_router = lax.psum(
        jnp.dot(tokens.T, d_logit, preferred_element_type=jnp.float32), ("dp", "expert")
    )
    grad_gate, grad_up, down_weight_gradient = weight_grads(
        expert_rows, hidden, expert_cot, d_pre_gate, d_pre_up
    )
    return (mixed, grad_tokens, grad_gate, grad_up, down_weight_gradient, grad_router)


def solution(mesh):
    placed = (
        P(("dp", "expert"), None),
        P(("dp", "expert"), None),
        P(("dp", "expert"), None, None),
        P(),
        P("expert", "dp", None),
        P("expert", "dp", None),
        P("expert", "dp", None),
    )
    return jax.shard_map(
        body,
        mesh=mesh,
        in_specs=placed,
        out_specs=(
            P(("dp", "expert"), None),
            P(("dp", "expert"), None),
            P("expert", "dp", None),
            P("expert", "dp", None),
            P("expert", "dp", None),
            P(),
        ),
        check_vma=False,
    )
```

profile of v0, /device:TPU:1, one launch (start us, length us, event | category | flops | bytes accessed | tf_op | source)
XLA Modules:
  0.0 655.6 jit_solution(1444224585253242615)
XLA Ops:
  8.0 0.7 all-gather.6.cloned.1.call-update
  9.4 0.8 shift-left_or_fusion
  10.4 2.9 gather_fusion
  13.3 9.6 %all-to-all-start = ((bf16[16,32,1536]{2,1,0:T(8,128)(2,1)}), bf16[16,32,1536]{2,1,0:T(8,128)(2,1)}, u32[]{:S(2)}, u32[]{:S(2)}) async-start(bf16[16,32,1536]{2,1,0:T(8,128)(2,1)} %bitcast.5), calls=%async_computation | async-start | bytes 3145728 | tf_op jit(solution)/shard_map/all_to_all | solution.py:62
  23.4 4.5 gather_fusion.2
  28.3 2.1 gather_fusion.1
  30.4 1.6 multiply_convert_fusion
  32.0 49.3 %all-to-all-done = bf16[16,32,1536]{2,1,0:T(8,128)(2,1)} async-done(((bf16[16,32,1536]{2,1,0:T(8,128)(2,1)}), bf16[16,32,1536]{2,1,0:T(8,128)(2,1)}, u32[]{:S(2)}, u32[]{:S(2)}) %all-to-all-start) | async-done | bytes 1572896 | tf_op jit(solution)/shard_map/all_to_all | solution.py:62
  81.2 4.5 all-to-all-start.2
  85.8 19.2 %all-gather.4.cloned.1.call-done = bf16[1,1536,1024]{2,1,0:T(8,128)(2,1)} async-done(((bf16[1,192,1024]{2,1,0:T(8,128)(2,1)}), bf16[1,1536,1024]{2,1,0:T(8,128)(2,1)}) %all-gather.4.cloned.1.call-update) | async-done | bytes 3145744 | tf_op jit(solution)/shard_map/all_gather | solution.py:58
  105.1 5.5 fusion.13
  110.6 69.9 %all-gather.6.cloned.1.call-done = bf16[1,1536,1024]{2,1,0:T(8,128)(2,1)} async-done(((bf16[1,192,1024]{2,1,0:T(8,128)(2,1)}), bf16[1,1536,1024]{2,1,0:T(8,128)(2,1)}) %all-gather.6.cloned.1.call-update) | async-done | bytes 3145744 | tf_op jit(solution)/shard_map/all_gather | solution.py:59
  180.5 5.5 fusion.9
  185.9 67.4 %all-gather.8.cloned.1.call-done = bf16[1,1024,1536]{2,1,0:T(8,128)(2,1)} async-done(((bf16[1,128,1536]{2,1,0:T(8,128)(2,1)}), bf16[1,1024,1536]{2,1,0:T(8,128)(2,1)}) %all-gather.8.cloned.1.call-update) | async-done | bytes 3145744 | tf_op jit(solution)/shard_map/all_gather | solution.py:60
  253.3 7.4 %multiply_convert_fusion.1 = (bf16[512,1024]{1,0:T(8,128)(2,1)}, bf16[512,1024]{1,0:T(8,128)(2,1)}, bf16[512,1024]{1,0:T(8,128)(2,1)S(1)}) fusion(f32[512,1024]{1,0:T(8,128)} %fusion.13, f32[512,1024]{1,0:T(8,128)} %fusion.9, bf16[512,1536]{1,0:T(8,128)(2,1)} %bitcast.18, bf16[1,1024,1536]{2,1,0:T(8,128)(2,1)} %all-gather.8.cloned.1.call-done), kind=kOutput, calls=%fused_computation.36 | convolution fusion | flops 1618477056 | bytes 12058624 | tf_op jit(solution)/shard_map/erd,ehd->erh/dot_general | solution.py:75
  260.7 1.1 copy-done.8
  261.8 4.9 fusion.1
  266.7 4.7 copy.104
  271.7 8.1 %fusion = bf16[1536,2048]{0,1:T(8,128)(2,1)} fusion(bf16[512,1536]{1,0:T(8,128)(2,1)} %bitcast.6, bf16[1,512,1024]{2,1,0:T(8,128)(2,1)} %bitcast.148, bf16[1,512,1024]{2,1,0:T(8,128)(2,1)} %bitcast.149), kind=kOutput, calls=%fused_computation.4 | convolution fusion | flops 3228565504 | bytes 9961472 | tf_op jit(solution)/shard_map/erc,erk->cek/dot_general | solution.py:22
  279.8 8.8 %copy.102 = bf16[1536,2048]{1,0:T(8,128)(2,1)} copy(bf16[1536,2048]{0,1:T(8,128)(2,1)} %fusion) | data formatting | bytes 12582912
  288.6 4.2 fusion.11
  292.8 1.8 fusion.22
  294.6 4.1 copy.126
  299.3 12.8 %reduce.2 = bf16[512,1536]{1,0:T(8,128)(2,1)} reduce(bf16[512,1,1536]{2,1,0:T(2,128)(2,1)} %bitcast.140, bf16[]{:T(256)} %broadcast.103), dimensions={1}, to_apply=%bitcast.134.reduce_sub_computation | reduce | bytes 3145730
  312.1 5.0 reshape.248
  317.1 7.9 %all-to-all-start.3 = ((bf16[16,2,24576]{2,1,0:T(2,128)(2,1)}), bf16[16,2,24576]{2,1,0:T(2,128)(2,1)}, u32[]{:S(2)}, u32[]{:S(2)}) async-start(bf16[16,2,24576]{2,1,0:T(2,128)(2,1)} %reshape.248), calls=%async_computation.3 | async-start | bytes 3145728 | tf_op jit(solution)/shard_map/all_to_all | solution.py:85
  325.0 4.0 fusion.25
  329.0 4.1 copy.127
  333.2 12.6 %reduce.1 = bf16[512,1536]{1,0:T(8,128)(2,1)} reduce(bf16[512,1,1536]{2,1,0:T(2,128)(2,1)} %bitcast.142, bf16[]{:T(256)} %broadcast.103), dimensions={1}, to_apply=%bitcast.135.reduce_sub_computation | reduce | bytes 3145730
  345.8 5.0 reshape.246
  350.7 12.6 %all-to-all-done.3 = bf16[16,2,24576]{2,1,0:T(2,128)(2,1)} async-done(((bf16[16,2,24576]{2,1,0:T(2,128)(2,1)}), bf16[16,2,24576]{2,1,0:T(2,128)(2,1)}, u32[]{:S(2)}, u32[]{:S(2)}) %all-to-all-start.3) | async-done | bytes 1572896 | tf_op jit(solution)/shard_map/all_to_all | solution.py:85
  363.3 4.6 all-to-all-start.1
  368.5 10.0 %reshape.249 = bf16[512,1,1536]{2,1,0:T(2,128)(2,1)} reshape(bf16[16,2,24576]{2,1,0:T(2,128)(2,1)} %all-to-all-done.3) | data formatting | bytes 3145728
  378.5 3.4 copy.106
  381.9 44.6 %all-to-all-done.1 = bf16[16,2,24576]{2,1,0:T(2,128)(2,1)} async-done(((bf16[16,2,24576]{2,1,0:T(2,128)(2,1)}), bf16[16,2,24576]{2,1,0:T(2,128)(2,1)}, u32[]{:S(2)}, u32[]{:S(2)}) %all-to-all-start.1) | async-done | bytes 1572896 | tf_op jit(solution)/shard_map/all_to_all | solution.py:72
  426.5 10.0 %reshape.247 = bf16[512,1,1536]{2,1,0:T(2,128)(2,1)} reshape(bf16[16,2,24576]{2,1,0:T(2,128)(2,1)} %all-to-all-done.1) | data formatting | bytes 3145728
  436.6 2.4 fusion.2
  439.6 0.9 convolution_bitcast_fusion
  440.9 1.3 fusion.29
  443.0 2.4 fusion.28
  445.5 1.2 copy.105
  446.8 1.1 copy.95
  447.9 54.7 %reduce-scatter.7.cloned.1.call-done = bf16[192,2048]{1,0:T(8,128)(2,1)} async-done(((bf16[1536,2048]{1,0:T(8,128)(2,1)}), bf16[192,2048]{1,0:T(8,128)(2,1)}) %reduce-scatter.7.cloned.1.call-update) | async-done | bytes 786448
  502.6 1.4 copy.103
  504.4 1.2 copy.93
  505.6 1.2 copy.94
  506.7 140.3 %all-reduce.2.cloned.1.call-done = f32[1536,16]{0,1:T(8,128)} async-done(((f32[1536,16]{0,1:T(8,128)}), f32[1536,16]{0,1:T(8,128)}) %all-reduce.2.cloned.1.call-update) | async-done | bytes 98320 | tf_op jit(solution)/shard_map/psum | solution.py:118
  647.0 1.5 copy.129
  (59 shorter events, 6.1 us)
Async XLA Ops:
  7.2 3.2 copy-start
  7.2 97.9 %all-gather.4.cloned.1.call-start = ((), (), s32[]{:S(2)}) async-start(), calls=%async_computation.6 | async-start | bytes 3538944 | tf_op jit(solution)/shard_map/all_gather | solution.py:58
  7.9 172.5 %all-gather.6.cloned.1.call-start = ((), (), s32[]{:S(2)}) async-start(), calls=%async_computation.7 | async-start | bytes 3538944 | tf_op jit(solution)/shard_map/all_gather | solution.py:59
  8.7 244.6 %all-gather.8.cloned.1.call-start = ((), (), s32[]{:S(2)}) async-start(), calls=%async_computation.8 | async-start | bytes 3538944 | tf_op jit(solution)/shard_map/all_gather | solution.py:60
  13.3 9.7 %copy-start.5 = (bf16[1536,16]{0,1:T(8,128)(2,1)S(1)}, bf16[1536,16]{0,1:T(8,128)(2,1)}, u32[]{:S(2)}) copy-start(bf16[1536,16]{0,1:T(8,128)(2,1)} %param.10) | copy-start | bytes 147460
  13.3 67.9 %all-to-all-start = ((bf16[16,32,1536]{2,1,0:T(8,128)(2,1)}), bf16[16,32,1536]{2,1,0:T(8,128)(2,1)}, u32[]{:S(2)}, u32[]{:S(2)}) async-start(bf16[16,32,1536]{2,1,0:T(8,128)(2,1)} %bitcast.5), calls=%async_computation | async-start | bytes 3145728 | tf_op jit(solution)/shard_map/all_to_all | solution.py:62
  23.4 4.7 copy-start.4
  23.4 4.8 copy-start.1
  81.2 104.7 %all-to-all-start.2 = ((bf16[16,32,1536]{2,1,0:T(8,128)(2,1)}), bf16[16,32,1536]{2,1,0:T(8,128)(2,1)}, u32[]{:S(2)}, u32[]{:S(2)}) async-start(bf16[16,32,1536]{2,1,0:T(8,128)(2,1)} %multiply_convert_fusion), calls=%async_computation.2 | async-start | bytes 3145728 | tf_op jit(solution)/shard_map/all_to_all | solution.py:73
  85.8 359.7 %reduce-scatter.9.cloned.1.call-start = ((), (), s32[]{:S(2)}) async-start(), calls=%async_computation.11 | async-start | bytes 3538944
  260.7 1.1 copy-start.8
  271.4 231.2 %reduce-scatter.7.cloned.1.call-start = ((), (), s32[]{:S(2)}) async-start(), calls=%async_computation.10 | async-start | bytes 7077888
  288.6 4.2 copy-start.6
  288.6 4.2 copy-start.7
  317.1 46.2 %all-to-all-start.3 = ((bf16[16,2,24576]{2,1,0:T(2,128)(2,1)}), bf16[16,2,24576]{2,1,0:T(2,128)(2,1)}, u32[]{:S(2)}, u32[]{:S(2)}) async-start(bf16[16,2,24576]{2,1,0:T(2,128)(2,1)} %reshape.248), calls=%async_computation.3 | async-start | bytes 3145728 | tf_op jit(solution)/shard_map/all_to_all | solution.py:85
  363.3 63.2 %all-to-all-start.1 = ((bf16[16,2,24576]{2,1,0:T(2,128)(2,1)}), bf16[16,2,24576]{2,1,0:T(2,128)(2,1)}, u32[]{:S(2)}, u32[]{:S(2)}) async-start(bf16[16,2,24576]{2,1,0:T(2,128)(2,1)} %reshape.246), calls=%async_computation.1 | async-start | bytes 3145728 | tf_op jit(solution)/shard_map/all_to_all | solution.py:72
  367.9 279.2 %all-reduce.2.cloned.1.call-start = ((), (), s32[]{:S(2)}) async-start(), calls=%async_computation.9 | async-start | bytes 196608 | tf_op jit(solution)/shard_map/psum | solution.py:118
  439.0 1.5 copy-start.3
  440.5 2.2 copy-start.2
Sparse Core Ops, SparseCore 0:
  9.7 95.3 all-gather.3
  106.7 73.7 all-gather.5
  182.1 71.1 all-gather.7
  271.6 79.1 reduce-scatter.8
  353.1 149.5 reduce-scatter.6
  507.8 139.2 all-reduce.1
where the time goes:
time: 665 us; the launch traced here: 656 us
  waiting for transfers between devices  460 us (69%)
  local copies, waits for them, and re-layouts  76 us (11%)
  matrix products  47.1 us (7%)
  other arithmetic  30.8 us (5%)
  starting transfers between devices  27 us (4%)
  between operations  14.5 us (2%)
    psum x1, waiting for transfers between devices, body(): lax.psum(jnp.dot(tokens.T, d_logit, preferred_element_type=jnp.float32),...  140 us
    all_gather x1, waiting for transfers between devices, body(): lax.all_gather(w_up, 'dp', axis=1, tiled=True)  69.9 us
    all_gather x1, waiting for transfers between devices, body(): lax.all_gather(w_down, 'dp', axis=1, tiled=True)  67.4 us
    unnamed x33, local copies, waits for them, and re-layouts  56.8 us
    unnamed x8, waiting for transfers between devices  56.8 us
    all_to_all x1, waiting for transfers between devices, body(): lax.all_to_all(picked, 'expert', split_axis=0, concat_axis=1, tiled=True)  49.3 us
    all_to_all x1, waiting for transfers between devices, body(): lax.all_to_all(expert_out, 'expert', split_axis=1, concat_axis=0, tiled=T...  44.6 us
    unnamed x2, other arithmetic  25.4 us
  transfers between devices with their start and end apart: 10, of which 8 were waited for; matrix products, arithmetic and copies ran while one was open for 20% of the time, Pallas kernels for 0%

commit v1 on v0

--- a/solution.py
+++ b/solution.py
@@ -57,7 +57,9 @@
     full_gate, full_up, full_down = (
         lax.all_gather(w_gate, "dp", axis=1, tiled=True),
         lax.all_gather(w_up, "dp", axis=1, tiled=True),
-        lax.all_gather(w_down, "dp", axis=1, tiled=True),
+        jnp.concatenate(
+            lax.all_to_all(jnp.stack([w_down] * lax.axis_size("dp")), "dp", 0, 0), axis=1
+        ),
     )
     expert_rows = lax.all_to_all(picked, "expert", split_axis=0, concat_axis=1, tiled=True)
     pre_gate = jnp.einsum(

time: 665 us -> 627 us (0.943)
  waiting for transfers between devices: 460 us -> 387 us
  blocking collectives: 0 us -> 33.5 us
    all_gather x1, waiting for transfers between devices: 69.9 us -> 0.02 us  [body(): lax.all_gather(w_up, 'dp', axis=1, tiled=True)]
    all_gather x1 -> x0, waiting for transfers between devices: 67.4 us -> none  [body(): lax.all_gather(w_down, 'dp', axis=1, tiled=True)]
    all_gather x1, waiting for transfers between devices: 19.2 us -> 77.5 us  [body(): lax.all_gather(w_gate, 'dp', axis=1, tiled=True)]
    all_to_all x1, waiting for transfers between devices: 0.01 us -> 55 us  [body(): lax.all_to_all(scaled_cot, 'expert', split_axis=0, concat_axis=1, tiled=T...]
    all_to_all x1, waiting for transfers between devices: 49.3 us -> 0.01 us  [body(): lax.all_to_all(jnp.stack([w_down] * lax.axis_size('dp')), 'dp', 0, 0)]
    all_to_all x0 -> x1, blocking collectives: none -> 33.5 us  [body(): lax.all_to_all(picked, 'expert', split_axis=0, concat_axis=1, tiled=True)]
    unnamed x8 -> x7, waiting for transfers between devices: 56.8 us -> 56.1 us
    unnamed x33 -> x35, local copies, waits for them, and re-layouts: 56.8 us -> 56.6 us
  transfers between devices with their start and end apart: 10 -> 9, of which waited for: 8 -> 6; matrix products, arithmetic and copies ran while one was open for 20% -> 22% of each run, Pallas kernels for 0% -> 0%
where the time goes in v1:
time: 627 us; the launch traced here: 618 us
  waiting for transfers between devices  387 us (62%)
  local copies, waits for them, and re-layouts  77.5 us (12%)
  matrix products  48 us (8%)
  blocking collectives  33.5 us (5%)
  other arithmetic  30.7 us (5%)
  starting transfers between devices  26.2 us (4%)
  between operations  14.2 us (2%)
    psum x1, waiting for transfers between devices, body(): lax.psum(jnp.dot(tokens.T, d_logit, preferred_element_type=jnp.float32),...  140 us
    all_gather x1, waiting for transfers between devices, body(): lax.all_gather(w_gate, 'dp', axis=1, tiled=True)  77.5 us
    unnamed x35, local copies, waits for them, and re-layouts  56.6 us
    unnamed x7, waiting for transfers between devices  56.1 us
    all_to_all x1, waiting for transfers between devices, body(): lax.all_to_all(scaled_cot, 'expert', split_axis=0, concat_axis=1, tiled=T...  55 us
    all_to_all x1, waiting for transfers between devices, body(): lax.all_to_all(expert_out, 'expert', split_axis=1, concat_axis=0, tiled=T...  44.8 us
    all_to_all x1, blocking collectives, body(): lax.all_to_all(picked, 'expert', split_axis=0, concat_axis=1, tiled=True)  33.5 us
    unnamed x2, other arithmetic  25.3 us
  transfers between devices with their start and end apart: 9, of which 6 were waited for; matrix products, arithmetic and copies ran while one was open for 22% of the time, Pallas kernels for 0%

profile of v1, /device:TPU:1, one launch (start us, length us, event | category | flops | bytes accessed | tf_op | source)
XLA Modules:
  0.0 617.7 jit_solution(9585926203435499738)
XLA Ops:
  8.7 0.8 shift-left_or_fusion
  9.6 1.1 fusion.30
  10.8 4.5 gather_fusion.2
  15.8 2.1 gather_fusion.1
  17.9 1.5 multiply_convert_fusion
  19.4 9.5 %all-to-all-start.3 = ((bf16[16,32,1536]{2,1,0:T(8,128)(2,1)}), bf16[16,32,1536]{2,1,0:T(8,128)(2,1)}, u32[]{:S(2)}, u32[]{:S(2)}) async-start(bf16[16,32,1536]{2,1,0:T(8,128)(2,1)} %multiply_convert_fusion), calls=%async_computation.3 | async-start | bytes 3145728 | tf_op jit(solution)/shard_map/all_to_all | solution.py:75
  28.9 2.9 gather_fusion
  31.8 55.0 %all-to-all-done.3 = bf16[16,32,1536]{2,1,0:T(8,128)(2,1)} async-done(((bf16[16,32,1536]{2,1,0:T(8,128)(2,1)}), bf16[16,32,1536]{2,1,0:T(8,128)(2,1)}, u32[]{:S(2)}, u32[]{:S(2)}) %all-to-all-start.3) | async-done | bytes 1572896 | tf_op jit(solution)/shard_map/all_to_all | solution.py:75
  86.8 33.5 %all_to_all.20 = bf16[16,32,1536]{2,1,0:T(8,128)(2,1)} all-to-all(bf16[16,32,1536]{2,1,0:T(8,128)(2,1)} %bitcast.137), channel_id=1, replica_groups=mesh['dp'=8,'expert'=16] {'expert'}, dimensions={0} | all-to-all | bytes 3145728 | tf_op jit(solution)/shard_map/all_to_all | solution.py:64
  120.3 1.9 stack.2
  122.3 4.5 all-to-all-start.1
  126.8 5.6 fusion.5
  132.4 77.5 %all-gather.3.cloned.1.call-done = bf16[1,1536,1024]{2,1,0:T(8,128)(2,1)} async-done(((bf16[1,192,1024]{2,1,0:T(8,128)(2,1)}), bf16[1,1536,1024]{2,1,0:T(8,128)(2,1)}) %all-gather.3.cloned.1.call-update) | async-done | bytes 3145744 | tf_op jit(solution)/shard_map/all_gather | solution.py:58
  209.9 5.5 fusion.9
  215.4 7.5 %multiply_convert_fusion.1 = (bf16[512,1024]{1,0:T(8,128)(2,1)}, bf16[512,1024]{1,0:T(8,128)(2,1)}, bf16[512,1024]{1,0:T(8,128)(2,1)S(1)}) fusion(f32[512,1024]{1,0:T(8,128)} %fusion.9, f32[512,1024]{1,0:T(8,128)} %fusion.5, bf16[512,1536]{1,0:T(8,128)(2,1)} %bitcast.19, bf16[1024,1536]{1,0:T(8,128)(2,1)} %bitcast.10), kind=kOutput, calls=%fused_computation.32 | convolution fusion | flops 1618477056 | bytes 12058624 | tf_op jit(solution)/shard_map/erd,ehd->erh/dot_general | solution.py:77
  222.9 1.0 copy-done.9
  223.8 4.9 fusion.1
  228.8 4.6 copy.104
  233.6 8.1 %fusion = bf16[1536,2048]{0,1:T(8,128)(2,1)} fusion(bf16[512,1536]{1,0:T(8,128)(2,1)} %bitcast.142, bf16[1,512,1024]{2,1,0:T(8,128)(2,1)} %bitcast.146, bf16[1,512,1024]{2,1,0:T(8,128)(2,1)} %bitcast.147), kind=kOutput, calls=%fused_computation.4 | convolution fusion | flops 3228565504 | bytes 9961472 | tf_op jit(solution)/shard_map/erc,erk->cek/dot_general | solution.py:22
  241.8 8.7 %copy.102 = bf16[1536,2048]{1,0:T(8,128)(2,1)} copy(bf16[1536,2048]{0,1:T(8,128)(2,1)} %fusion) | data formatting | bytes 12582912
  250.5 4.2 fusion.7
  254.8 1.8 fusion.16
  256.6 4.1 copy.126
  261.2 12.8 %reduce.2 = bf16[512,1536]{1,0:T(8,128)(2,1)} reduce(bf16[512,1,1536]{2,1,0:T(2,128)(2,1)} %bitcast.133, bf16[]{:T(256)} %broadcast.106), dimensions={1}, to_apply=%bitcast.127.reduce_sub_computation | reduce | bytes 3145730
  274.0 5.0 reshape.254
  278.9 7.2 %all-to-all-start.4 = ((bf16[16,2,24576]{2,1,0:T(2,128)(2,1)}), bf16[16,2,24576]{2,1,0:T(2,128)(2,1)}, u32[]{:S(2)}, u32[]{:S(2)}) async-start(bf16[16,2,24576]{2,1,0:T(2,128)(2,1)} %reshape.254), calls=%async_computation.4 | async-start | bytes 3145728 | tf_op jit(solution)/shard_map/all_to_all | solution.py:87
  286.1 4.0 fusion.15
  290.1 4.1 copy.127
  294.2 12.6 %reduce.1 = bf16[512,1536]{1,0:T(8,128)(2,1)} reduce(bf16[512,1,1536]{2,1,0:T(2,128)(2,1)} %bitcast.135, bf16[]{:T(256)} %broadcast.106), dimensions={1}, to_apply=%bitcast.128.reduce_sub_computation | reduce | bytes 3145730
  306.8 5.0 reshape.252
  311.7 13.7 %all-to-all-done.4 = bf16[16,2,24576]{2,1,0:T(2,128)(2,1)} async-done(((bf16[16,2,24576]{2,1,0:T(2,128)(2,1)}), bf16[16,2,24576]{2,1,0:T(2,128)(2,1)}, u32[]{:S(2)}, u32[]{:S(2)}) %all-to-all-start.4) | async-done | bytes 1572896 | tf_op jit(solution)/shard_map/all_to_all | solution.py:87
  325.4 4.7 all-to-all-start.2
  330.8 10.0 %reshape.255 = bf16[512,1,1536]{2,1,0:T(2,128)(2,1)} reshape(bf16[16,2,24576]{2,1,0:T(2,128)(2,1)} %all-to-all-done.4) | data formatting | bytes 3145728
  340.8 3.3 copy.106
  344.2 44.8 %all-to-all-done.2 = bf16[16,2,24576]{2,1,0:T(2,128)(2,1)} async-done(((bf16[16,2,24576]{2,1,0:T(2,128)(2,1)}), bf16[16,2,24576]{2,1,0:T(2,128)(2,1)}, u32[]{:S(2)}, u32[]{:S(2)}) %all-to-all-start.2) | async-done | bytes 1572896 | tf_op jit(solution)/shard_map/all_to_all | solution.py:74
  389.0 10.0 %reshape.253 = bf16[512,1,1536]{2,1,0:T(2,128)(2,1)} reshape(bf16[16,2,24576]{2,1,0:T(2,128)(2,1)} %all-to-all-done.2) | data formatting | bytes 3145728
  399.0 2.4 fusion.2
  402.1 0.9 convolution_bitcast_fusion
  403.3 1.3 fusion.20
  405.4 2.4 fusion.19
  407.9 1.2 copy.105
  409.2 1.1 copy.95
  410.3 54.7 %reduce-scatter.7.cloned.1.call-done = bf16[192,2048]{1,0:T(8,128)(2,1)} async-done(((bf16[1536,2048]{1,0:T(8,128)(2,1)}), bf16[192,2048]{1,0:T(8,128)(2,1)}) %reduce-scatter.7.cloned.1.call-update) | async-done | bytes 786448
  465.0 1.4 copy.103
  466.8 1.2 copy.93
  468.0 1.2 copy.94
  469.2 140.3 %all-reduce.2.cloned.1.call-done = f32[1536,16]{0,1:T(8,128)} async-done(((f32[1536,16]{0,1:T(8,128)}), f32[1536,16]{0,1:T(8,128)}) %all-reduce.2.cloned.1.call-update) | async-done | bytes 98320 | tf_op jit(solution)/shard_map/psum | solution.py:120
  609.4 1.5 copy.129
  (60 shorter events, 5.7 us)
Async XLA Ops:
  7.2 2.5 copy-start
  7.2 119.6 %all-gather.5.cloned.1.call-start = ((), (), s32[]{:S(2)}) async-start(), calls=%async_computation.8 | async-start | bytes 3538944 | tf_op jit(solution)/shard_map/all_gather | solution.py:59
  7.9 202.0 %all-gather.3.cloned.1.call-start = ((), (), s32[]{:S(2)}) async-start(), calls=%async_computation.7 | async-start | bytes 3538944 | tf_op jit(solution)/shard_map/all_gather | solution.py:58
  10.8 4.7 copy-start.5
  10.8 5.0 copy-start.1
  19.4 67.4 %all-to-all-start.3 = ((bf16[16,32,1536]{2,1,0:T(8,128)(2,1)}), bf16[16,32,1536]{2,1,0:T(8,128)(2,1)}, u32[]{:S(2)}, u32[]{:S(2)}) async-start(bf16[16,32,1536]{2,1,0:T(8,128)(2,1)} %multiply_convert_fusion), calls=%async_computation.3 | async-start | bytes 3145728 | tf_op jit(solution)/shard_map/all_to_all | solution.py:75
  31.8 88.5 %copy-start.4 = (bf16[1,128,1536]{2,1,0:T(8,128)(2,1)S(1)}, bf16[1,128,1536]{2,1,0:T(8,128)(2,1)}, u32[]{:S(2)}) copy-start(bf16[1,128,1536]{2,1,0:T(8,128)(2,1)} %param.13) | copy-start | bytes 1179652
  122.3 93.1 %all-to-all-start.1 = ((bf16[8,1,128,1536]{3,2,1,0:T(8,128)(2,1)}), bf16[8,1,128,1536]{3,2,1,0:T(8,128)(2,1)}, u32[]{:S(2)}, u32[]{:S(2)}) async-start(bf16[8,1,128,1536]{3,2,1,0:T(8,128)(2,1)} %stack.2), calls=%async_computation.1 | async-start | bytes 6291456 | tf_op jit(solution)/shard_map/all_to_all | solution.py:61
  126.8 281.1 %reduce-scatter.9.cloned.1.call-start = ((), (), s32[]{:S(2)}) async-start(), calls=%async_computation.11 | async-start | bytes 3538944
  222.9 1.0 copy-start.9
  233.4 231.6 %reduce-scatter.7.cloned.1.call-start = ((), (), s32[]{:S(2)}) async-start(), calls=%async_computation.10 | async-start | bytes 7077888
  250.5 4.2 copy-start.7
  250.5 4.2 copy-start.8
  278.9 46.5 %all-to-all-start.4 = ((bf16[16,2,24576]{2,1,0:T(2,128)(2,1)}), bf16[16,2,24576]{2,1,0:T(2,128)(2,1)}, u32[]{:S(2)}, u32[]{:S(2)}) async-start(bf16[16,2,24576]{2,1,0:T(2,128)(2,1)} %reshape.254), calls=%async_computation.4 | async-start | bytes 3145728 | tf_op jit(solution)/shard_map/all_to_all | solution.py:87
  325.4 63.5 %all-to-all-start.2 = ((bf16[16,2,24576]{2,1,0:T(2,128)(2,1)}), bf16[16,2,24576]{2,1,0:T(2,128)(2,1)}, u32[]{:S(2)}, u32[]{:S(2)}) async-start(bf16[16,2,24576]{2,1,0:T(2,128)(2,1)} %reshape.252), calls=%async_computation.2 | async-start | bytes 3145728 | tf_op jit(solution)/shard_map/all_to_all | solution.py:74
  330.1 279.3 %all-reduce.2.cloned.1.call-start = ((), (), s32[]{:S(2)}) async-start(), calls=%async_computation.9 | async-start | bytes 196608 | tf_op jit(solution)/shard_map/psum | solution.py:120
  401.4 1.5 copy-start.3
  401.9 1.4 copy-start.6
  402.9 2.2 copy-start.2
Sparse Core Ops, SparseCore 0:
  9.7 93.4 all-gather.4
  104.8 105.0 all-gather.2
  233.5 79.8 reduce-scatter.8
  315.7 149.2 reduce-scatter.6
  470.2 139.2 all-reduce.1
